TPU v7x, 512 devices: a whole 4x8x8 slice. The times are simulated.
512 devices in a mesh: ctx: 64 (over z_lo, y, core), ch: 8 (over z_hi, x).
Axes of the slice: x: 4, y: 8, z: 8 (z_hi: 2, z_lo: 4; z = z_hi * 4 + z_lo), core: 2. Of those that a mesh axis runs over, the one named last changes fastest.
Arguments:
- cotangent: bfloat16 [8192, 4096], P('ctx', 'ch'), may hold values from -6 to 6
- out_weight: bfloat16 [4096, 4096], P('ch', 'ctx'), may hold values from -0.09375 to 0.09375
- gate_value: float32 [8192, 4096], P('ctx', 'ch'), may hold values from -6 to 6
- conv_output: float32 [8192, 4096], P('ctx', 'ch'), may hold values from -6 to 6
- conv_input: float32 [8192, 4096], P('ctx', 'ch'), may hold values from -6 to 6
- filters: float32 [256, 2048], P('ch'), may hold values from -1 to 1
Outputs:
- input_grad: float32 [8192, 4096], P('ctx', 'ch')
- gate_grad: float32 [8192, 4096], P('ctx', 'ch')
- filter_grad: float32 [256, 2048], P('ch', 'ctx')
All inputs are finite; a program needn't handle non-finite values.
Results may differ from a plain program's by a relative error of at most 0.0003.
Values may be sent and summed in bfloat16 or wider, within the bound.
A program may use at most 64 MiB of HBM per device.

v0:
```python
import math

import jax
import jax.numpy as jnp
from jax import lax
from jax.sharding import PartitionSpec as P

exact_mode = lax.Precision.HIGHEST


def shifted(block, axis, distance):
    devices = range(lax.axis_size(axis))
    route = [(i - distance, i) for i in devices if i - distance in devices]
    return lax.ppermute(block, axis, route)


def spectral_tables(tok_rows):
    length = 2 * tok_rows
    frequency = jnp.arange(length, dtype=jnp.int32)
    angles = (frequency[:, None] * frequency[None, :] % length).astype(jnp.float32) * (
        2.0 * math.pi / length
    )
    cosine = jnp.cos(angles)
    sine_part = jnp.sin(angles)
    forward = jnp.concatenate([cosine, -sine_part], axis=0)
    inverse = jnp.concatenate([cosine, -sine_part], axis=1) / length
    return (forward, inverse)


def spectrum_step(
    spectra, shard_block, offset, forward_rows, filter_spectra, input_spectrum, groups
):
    running, lag_spectra = spectra
    freq_count = forward_rows.shape[0] // 2
    channels = shard_block.shape[1]
    per_group = channels // groups
    block_spectrum = jnp.dot(forward_rows, shard_block, precision=exact_mode)
    filter_block = lax.dynamic_index_in_dim(filter_spectra, offset, 0, keepdims=False)
    block_real = block_spectrum[:freq_count].reshape(freq_count, groups, per_group)
    block_imag = block_spectrum[freq_count:].reshape(freq_count, groups, per_group)
    filter_real = filter_block[:freq_count][:, :, None]
    filter_imag = filter_block[freq_count:][:, :, None]
    input_real = input_spectrum[:freq_count].reshape(freq_count, groups, per_group)
    input_imag = input_spectrum[freq_count:].reshape(freq_count, groups, per_group)
    prod_real = block_real * filter_real + block_imag * filter_imag
    prod_imag = block_imag * filter_real - block_real * filter_imag
    running = running + jnp.concatenate([prod_real, prod_imag], axis=0).reshape(
        2 * freq_count, channels
    )
    cross_real = jnp.sum(block_real * input_real + block_imag * input_imag, axis=2)
    cross_imag = jnp.sum(block_imag * input_real - block_real * input_imag, axis=2)
    cross_spectrum = jnp.concatenate([cross_real, cross_imag], axis=0)
    lag_spectra = lax.dynamic_update_index_in_dim(lag_spectra, cross_spectrum, offset, 0)
    return (running, lag_spectra)


def shards(cotangent, out_weight, gate_value, conv_output, conv_input, filters):
    tok_rows, channels = gate_value.shape
    groups, lag_count = filters.shape
    ahead_blocks = lag_count // tok_rows
    spectrum_len = 2 * tok_rows
    full_cotangent = lax.all_gather(cotangent, "ch", axis=1, tiled=True)
    grad_out = lax.dot_general(
        full_cotangent,
        lax.all_gather(out_weight, "ctx", axis=1, tiled=True),
        (((1,), (1,)), ((), ())),
        preferred_element_type=jnp.float32,
    )
    gate_grad = grad_out * conv_output
    seq_grad = grad_out * gate_value
    forward_full, inverse_full = spectral_tables(tok_rows)
    forward_rows = forward_full[:, :tok_rows]
    blocks = filters.reshape(groups, ahead_blocks, tok_rows)
    border = jnp.zeros((groups, 1, tok_rows), jnp.float32)
    padded = jnp.concatenate([border, blocks, border], axis=1)
    segments = jnp.concatenate([padded[:, 1:], padded[:, :-1]], axis=2)
    filter_spectra = jnp.einsum("gdn,fn->dfg", segments, forward_full, precision=exact_mode)
    input_spectrum = jnp.dot(forward_rows, conv_input, precision=exact_mode)

    def absorb(spectra, shard_block, offset):
        return spectrum_step(
            spectra, shard_block, offset, forward_rows, filter_spectra, input_spectrum, groups
        )

    spectra = (
        jnp.zeros((2 * spectrum_len, channels), jnp.float32),
        jnp.zeros((ahead_blocks + 1, 2 * spectrum_len, groups), jnp.float32),
    )
    spectra = absorb(spectra, seq_grad, 0)

    def relay_step(carried, offset):
        shard_block, inner_state = carried
        shard_block = shifted(shard_block, "ctx", -1)
        return ((shard_block, absorb(inner_state, shard_block, offset)), None)

    (last_block, spectra), unused = lax.scan(
        relay_step, (seq_grad, spectra), jnp.arange(1, ahead_blocks + 1, dtype=jnp.int32)
    )
    running, lag_spectra = spectra
    input_grad = jnp.dot(inverse_full[:tok_rows], running, precision=exact_mode)
    lag_terms = jnp.einsum("mf,dfg->dmg", inverse_full, lag_spectra, precision=exact_mode)
    joined = lag_terms[:ahead_blocks, :tok_rows] + lag_terms[1:, tok_rows:]
    tokens = tok_rows * lax.axis_size("ctx")
    per_group = channels // groups
    partial_sums = joined.transpose(2, 0, 1).reshape(groups, lag_count) * (
        1.0 / math.sqrt(per_group * tokens)
    )
    filter_grad = lax.psum_scatter(partial_sums, "ctx", scatter_dimension=1, tiled=True)
    return (input_grad, gate_grad, filter_grad)


def solution(mesh):
    return jax.shard_map(
        shards,
        mesh=mesh,
        in_specs=(
            P("ctx", "ch"),
            P("ch", "ctx"),
            P("ctx", "ch"),
            P("ctx", "ch"),
            P("ctx", "ch"),
            P("ch", None),
        ),
        out_specs=(P("ctx", "ch"), P("ctx", "ch"), P("ch", "ctx")),
        check_vma=False,
    )
```

profile of v0, /device:TPU:1, one launch (start us, length us, event | category | flops | bytes accessed | tf_op | source)
XLA Modules:
  0.0 705.0 jit_solution(1551357461140330454)
XLA Ops:
  8.7 1.0 sine_negate_fusion
  9.8 1.1 fusion.3
  11.9 1.0 fusion.32
  13.0 69.1 %all-gather.3.cloned.1.call-done = bf16[128,4096]{1,0:T(8,128)(2,1)} async-done(((bf16[128,512]{1,0:T(8,128)(2,1)}), bf16[128,4096]{1,0:T(8,128)(2,1)}) %all-gather.3.cloned.1.call-update) | async-done | bytes 1048592 | tf_op jit(solution)/shard_map/all_gather | solution.py:62
  82.1 120.1 %all-gather.5.cloned.1.call-done = bf16[512,4096]{0,1:T(8,128)(2,1)} async-done(((bf16[512,64]{0,1:T(8,128)(2,1)}), bf16[512,4096]{0,1:T(8,128)(2,1)}) %all-gather.5.cloned.1.call-update) | async-done | bytes 4194320 | tf_op jit(solution)/shard_map/all_gather | solution.py:65
  202.2 3.9 fusion.29
  206.2 1.0 fusion.31
  207.8 1.1 dynamic_update_slice.8
  208.9 175.1 %while.14 = (s32[]{:T(128)}, f32[128,512]{1,0:T(8,128)}, f32[512,512]{0,1:T(8,128)S(1)}, f32[17,512,32]{1,2,0:T(8,128)}, f32[512,128]{1,0:T(8,128)S(1)}, /*index...) while((s32[]{:T(128)}, f32[128,512]{1,0:T(8,128)}, ...), condition=%wide.region_5.6_spmd, body=%wide.region_2.5_spmd.sunk | while | flops 405012480 | bytes 10879211 | solution.py:96
  208.9 2.2 collective-permute-start
  214.7 2.2 collective-permute-done
  219.9 1.9 collective-permute-start
  225.3 2.4 collective-permute-done
  230.8 1.9 collective-permute-start
  236.3 2.4 collective-permute-done
  241.8 1.9 collective-permute-start
  247.2 2.4 collective-permute-done
  252.7 1.9 collective-permute-start
  258.2 2.4 collective-permute-done
  263.6 1.9 collective-permute-start
  269.1 2.4 collective-permute-done
  274.6 1.9 collective-permute-start
  280.0 2.4 collective-permute-done
  285.5 1.9 collective-permute-start
  291.0 2.4 collective-permute-done
  296.5 1.9 collective-permute-start
  301.9 2.4 collective-permute-done
  307.4 1.9 collective-permute-start
  312.8 2.4 collective-permute-done
  315.3 1.0 fusion.51
  318.3 1.9 collective-permute-start
  323.8 2.4 collective-permute-done
  329.3 1.9 collective-permute-start
  334.7 2.4 collective-permute-done
  340.2 1.9 collective-permute-start
  345.7 2.4 collective-permute-done
  351.2 1.9 collective-permute-start
  356.6 2.4 collective-permute-done
  359.1 1.0 fusion.51
  362.1 1.9 collective-permute-start
  367.6 2.4 collective-permute-done
  373.0 1.9 collective-permute-start
  378.5 2.4 collective-permute-done
  384.0 2.3 convolution_bitcast_fusion
  386.4 1.3 copy.19
  387.8 1.9 fusion.20
  389.7 307.4 %reduce-scatter.4.cloned.1.call-done = f32[32,32]{1,0:T(8,128)} async-done(((f32[2048,32]{1,0:T(8,128)}), f32[32,32]{1,0:T(8,128)}) %reduce-scatter.4.cloned.1.call-update) | async-done | bytes 4112
  697.0 1.4 copy.18
  (155 shorter events, 72.8 us)
Async XLA Ops:
  7.2 4.8 copy-start
  7.2 2.6 copy-start.5
  7.2 74.9 %all-gather.3.cloned.1.call-start = ((), (), s32[]{:S(2)}) async-start(), calls=%async_computation.1 | async-start | bytes 1179648 | tf_op jit(solution)/shard_map/all_gather | solution.py:62
  7.9 194.3 %all-gather.5.cloned.1.call-start = ((), (), s32[]{:S(2)}) async-start(), calls=%async_computation.2 | async-start | bytes 4259840 | tf_op jit(solution)/shard_map/all_gather | solution.py:65
  8.7 688.4 %reduce-scatter.4.cloned.1.call-start = ((), (), s32[]{:S(2)}) async-start(), calls=%async_computation.3 | async-start | bytes 1064960
  10.9 1.0 copy-start.1
  11.0 191.3 %copy-start.3 = (f32[128,512]{1,0:T(8,128)S(1)}, f32[128,512]{1,0:T(8,128)}, u32[]{:S(2)}) copy-start(f32[128,512]{1,0:T(8,128)} %param.11) | copy-start | bytes 786436
  11.0 191.3 %copy-start.4 = (f32[128,512]{1,0:T(8,128)S(1)}, f32[128,512]{1,0:T(8,128)}, u32[]{:S(2)}) copy-start(f32[128,512]{1,0:T(8,128)} %param.10) | copy-start | bytes 786436
  206.2 1.3 copy-start.2
  208.9 7.9 %collective-permute-start = (f32[128,512]{1,0:T(8,128)}, f32[128,512]{1,0:T(8,128)S(1)}, u32[]{:S(2)}, u32[]{:S(2)}) collective-permute-start(f32[128,512]{1,0:T(8,128)} %get-tuple-element.155), channel_id=1, source_target_pairs={{8,0},{16,8},{24,16},{32,24},{40,32},{48,40},{56,48},{64,56},{72,6... | collective-permute-start | bytes 786440 | tf_op jit(solution)/shard_map/while/body/eval_jaxpr/ppermute | solution.py:14
  219.9 7.9 %collective-permute-start = (f32[128,512]{1,0:T(8,128)}, f32[128,512]{1,0:T(8,128)S(1)}, u32[]{:S(2)}, u32[]{:S(2)}) collective-permute-start(f32[128,512]{1,0:T(8,128)} %get-tuple-element.155), channel_id=1, source_target_pairs={{8,0},{16,8},{24,16},{32,24},{40,32},{48,40},{56,48},{64,56},{72,6... | collective-permute-start | bytes 786440 | tf_op jit(solution)/shard_map/while/body/eval_jaxpr/ppermute | solution.py:14
  230.8 7.9 %collective-permute-start = (f32[128,512]{1,0:T(8,128)}, f32[128,512]{1,0:T(8,128)S(1)}, u32[]{:S(2)}, u32[]{:S(2)}) collective-permute-start(f32[128,512]{1,0:T(8,128)} %get-tuple-element.155), channel_id=1, source_target_pairs={{8,0},{16,8},{24,16},{32,24},{40,32},{48,40},{56,48},{64,56},{72,6... | collective-permute-start | bytes 786440 | tf_op jit(solution)/shard_map/while/body/eval_jaxpr/ppermute | solution.py:14
  241.8 7.9 %collective-permute-start = (f32[128,512]{1,0:T(8,128)}, f32[128,512]{1,0:T(8,128)S(1)}, u32[]{:S(2)}, u32[]{:S(2)}) collective-permute-start(f32[128,512]{1,0:T(8,128)} %get-tuple-element.155), channel_id=1, source_target_pairs={{8,0},{16,8},{24,16},{32,24},{40,32},{48,40},{56,48},{64,56},{72,6... | collective-permute-start | bytes 786440 | tf_op jit(solution)/shard_map/while/body/eval_jaxpr/ppermute | solution.py:14
  252.7 7.9 %collective-permute-start = (f32[128,512]{1,0:T(8,128)}, f32[128,512]{1,0:T(8,128)S(1)}, u32[]{:S(2)}, u32[]{:S(2)}) collective-permute-start(f32[128,512]{1,0:T(8,128)} %get-tuple-element.155), channel_id=1, source_target_pairs={{8,0},{16,8},{24,16},{32,24},{40,32},{48,40},{56,48},{64,56},{72,6... | collective-permute-start | bytes 786440 | tf_op jit(solution)/shard_map/while/body/eval_jaxpr/ppermute | solution.py:14
  263.6 7.9 %collective-permute-start = (f32[128,512]{1,0:T(8,128)}, f32[128,512]{1,0:T(8,128)S(1)}, u32[]{:S(2)}, u32[]{:S(2)}) collective-permute-start(f32[128,512]{1,0:T(8,128)} %get-tuple-element.155), channel_id=1, source_target_pairs={{8,0},{16,8},{24,16},{32,24},{40,32},{48,40},{56,48},{64,56},{72,6... | collective-permute-start | bytes 786440 | tf_op jit(solution)/shard_map/while/body/eval_jaxpr/ppermute | solution.py:14
  274.6 7.9 %collective-permute-start = (f32[128,512]{1,0:T(8,128)}, f32[128,512]{1,0:T(8,128)S(1)}, u32[]{:S(2)}, u32[]{:S(2)}) collective-permute-start(f32[128,512]{1,0:T(8,128)} %get-tuple-element.155), channel_id=1, source_target_pairs={{8,0},{16,8},{24,16},{32,24},{40,32},{48,40},{56,48},{64,56},{72,6... | collective-permute-start | bytes 786440 | tf_op jit(solution)/shard_map/while/body/eval_jaxpr/ppermute | solution.py:14
  285.5 7.9 %collective-permute-start = (f32[128,512]{1,0:T(8,128)}, f32[128,512]{1,0:T(8,128)S(1)}, u32[]{:S(2)}, u32[]{:S(2)}) collective-permute-start(f32[128,512]{1,0:T(8,128)} %get-tuple-element.155), channel_id=1, source_target_pairs={{8,0},{16,8},{24,16},{32,24},{40,32},{48,40},{56,48},{64,56},{72,6... | collective-permute-start | bytes 786440 | tf_op jit(solution)/shard_map/while/body/eval_jaxpr/ppermute | solution.py:14
  296.5 7.9 %collective-permute-start = (f32[128,512]{1,0:T(8,128)}, f32[128,512]{1,0:T(8,128)S(1)}, u32[]{:S(2)}, u32[]{:S(2)}) collective-permute-start(f32[128,512]{1,0:T(8,128)} %get-tuple-element.155), channel_id=1, source_target_pairs={{8,0},{16,8},{24,16},{32,24},{40,32},{48,40},{56,48},{64,56},{72,6... | collective-permute-start | bytes 786440 | tf_op jit(solution)/shard_map/while/body/eval_jaxpr/ppermute | solution.py:14
  307.4 7.9 %collective-permute-start = (f32[128,512]{1,0:T(8,128)}, f32[128,512]{1,0:T(8,128)S(1)}, u32[]{:S(2)}, u32[]{:S(2)}) collective-permute-start(f32[128,512]{1,0:T(8,128)} %get-tuple-element.155), channel_id=1, source_target_pairs={{8,0},{16,8},{24,16},{32,24},{40,32},{48,40},{56,48},{64,56},{72,6... | collective-permute-start | bytes 786440 | tf_op jit(solution)/shard_map/while/body/eval_jaxpr/ppermute | solution.py:14
  318.3 7.9 %collective-permute-start = (f32[128,512]{1,0:T(8,128)}, f32[128,512]{1,0:T(8,128)S(1)}, u32[]{:S(2)}, u32[]{:S(2)}) collective-permute-start(f32[128,512]{1,0:T(8,128)} %get-tuple-element.155), channel_id=1, source_target_pairs={{8,0},{16,8},{24,16},{32,24},{40,32},{48,40},{56,48},{64,56},{72,6... | collective-permute-start | bytes 786440 | tf_op jit(solution)/shard_map/while/body/eval_jaxpr/ppermute | solution.py:14
  329.3 7.9 %collective-permute-start = (f32[128,512]{1,0:T(8,128)}, f32[128,512]{1,0:T(8,128)S(1)}, u32[]{:S(2)}, u32[]{:S(2)}) collective-permute-start(f32[128,512]{1,0:T(8,128)} %get-tuple-element.155), channel_id=1, source_target_pairs={{8,0},{16,8},{24,16},{32,24},{40,32},{48,40},{56,48},{64,56},{72,6... | collective-permute-start | bytes 786440 | tf_op jit(solution)/shard_map/while/body/eval_jaxpr/ppermute | solution.py:14
  340.2 7.9 %collective-permute-start = (f32[128,512]{1,0:T(8,128)}, f32[128,512]{1,0:T(8,128)S(1)}, u32[]{:S(2)}, u32[]{:S(2)}) collective-permute-start(f32[128,512]{1,0:T(8,128)} %get-tuple-element.155), channel_id=1, source_target_pairs={{8,0},{16,8},{24,16},{32,24},{40,32},{48,40},{56,48},{64,56},{72,6... | collective-permute-start | bytes 786440 | tf_op jit(solution)/shard_map/while/body/eval_jaxpr/ppermute | solution.py:14
  351.2 7.9 %collective-permute-start = (f32[128,512]{1,0:T(8,128)}, f32[128,512]{1,0:T(8,128)S(1)}, u32[]{:S(2)}, u32[]{:S(2)}) collective-permute-start(f32[128,512]{1,0:T(8,128)} %get-tuple-element.155), channel_id=1, source_target_pairs={{8,0},{16,8},{24,16},{32,24},{40,32},{48,40},{56,48},{64,56},{72,6... | collective-permute-start | bytes 786440 | tf_op jit(solution)/shard_map/while/body/eval_jaxpr/ppermute | solution.py:14
  362.1 7.9 %collective-permute-start = (f32[128,512]{1,0:T(8,128)}, f32[128,512]{1,0:T(8,128)S(1)}, u32[]{:S(2)}, u32[]{:S(2)}) collective-permute-start(f32[128,512]{1,0:T(8,128)} %get-tuple-element.155), channel_id=1, source_target_pairs={{8,0},{16,8},{24,16},{32,24},{40,32},{48,40},{56,48},{64,56},{72,6... | collective-permute-start | bytes 786440 | tf_op jit(solution)/shard_map/while/body/eval_jaxpr/ppermute | solution.py:14
  373.0 7.9 %collective-permute-start = (f32[128,512]{1,0:T(8,128)}, f32[128,512]{1,0:T(8,128)S(1)}, u32[]{:S(2)}, u32[]{:S(2)}) collective-permute-start(f32[128,512]{1,0:T(8,128)} %get-tuple-element.155), channel_id=1, source_target_pairs={{8,0},{16,8},{24,16},{32,24},{40,32},{48,40},{56,48},{64,56},{72,6... | collective-permute-start | bytes 786440 | tf_op jit(solution)/shard_map/while/body/eval_jaxpr/ppermute | solution.py:14
Sparse Core Ops, SparseCore 0:
  11.1 71.0 all-gather.2
  84.3 117.9 all-gather.4
  387.8 309.1 reduce-scatter.3
where the time goes:
time: 711 us; the launch traced here: 705 us
  waiting for transfers between devices  537 us (76%)
  local copies, waits for them, and re-layouts  39.4 us (6%)
  loops' own time  33.8 us (5%)
  starting transfers between devices  30.9 us (4%)
  matrix products  27.7 us (4%)
  other arithmetic  22.5 us (3%)
  between operations  13.9 us (2%)
    unnamed x4, waiting for transfers between devices  309 us
    all_gather x1, waiting for transfers between devices, shards(): lax.all_gather(out_weight, 'ctx', axis=1, tiled=True)  120 us
    all_gather x1, waiting for transfers between devices, shards(): full_cotangent = lax.all_gather(cotangent, 'ch', axis=1, tiled=True)  69.1 us
    ppermute x16, waiting for transfers between devices, shifted(): return lax.ppermute(block, axis, route)  38.8 us
    another operation x1, loops' own time, shards(): lax.scan(relay_step, (seq_grad, spectra), jnp.arange(1, ahead_blocks + 1,...  33.8 us
    ppermute x16, starting transfers between devices, shifted(): return lax.ppermute(block, axis, route)  30.8 us
    dot_general x17, matrix products, spectrum_step(): block_spectrum = jnp.dot(forward_rows, shard_block, precision=exact_mode)  17.4 us
  transfers between devices with their start and end apart: 19, of which 19 were waited for; matrix products, arithmetic and copies ran while one was open for 4% of the time, Pallas kernels for 0%

commit v1 on v0

v1 whole, which is shorter than its diff:
```python
import functools
import math

import jax
import jax.numpy as jnp
from jax import lax
from jax.experimental import pallas as pl
from jax.experimental.pallas import tpu as pltpu
from jax.sharding import PartitionSpec as P

MESH = pl.DeviceIdType.MESH
F32, BF16 = jnp.float32, jnp.bfloat16
NT = (((1,), (1,)), ((), ()))
NN = (((1,), (0,)), ((), ()))
GRID = {"z_lo": 4, "y": 8, "z_hi": 2, "x": 4}
TOK = 128
BLOCK = 2 * TOK
ROWS = 8


def split(value):
    high = value.astype(BF16)
    return high, (value - high.astype(F32)).astype(BF16)


def mm(a, b, dims):
    return lax.dot_general(a, b, dims, preferred_element_type=F32)


def mm3(a, b, dims):
    return mm(a[0], b[0], dims) + (mm(a[0], b[1], dims) + mm(a[1], b[0], dims))


def kernel(
    dims, scale,
    cot_ref, w_ref, gate_ref, cout_ref, cin_ref, filt_ref,
    ig_ref, gg_ref, fg_ref,
    wfull, cotfull, xt, xb, st, sb, outt, rt, tap_hi, tap_lo, xr_hi, xr_lo, corr, fgs, fgr, grad,
    w_send, w_recv, c_send, c_recv, x_sem, s_sem, o_sem, f_sem,
):
    zl_n, y_n, zh_n, x_n, lag_blocks = dims
    chips = zl_n * y_n
    n_ctx = 2 * chips
    me = lax.axis_index("ctx")
    core = lax.rem(me, 2)
    chip = lax.div(me, 2)
    y = lax.rem(chip, y_n)
    zl = lax.div(chip, y_n)
    mej = lax.axis_index("ch")
    x = lax.rem(mej, x_n)
    zh = lax.div(mej, x_n)
    sibling = me + 1 - 2 * core
    x_near = ([lax.rem(x + 1, x_n), lax.rem(x + x_n - 1, x_n)] if x_n > 1 else [])

    def ctx_of(z_, y_, c_):
        return (z_ * y_n + y_) * 2 + c_

    def remote(src, dst, send, recv, **where):
        return pltpu.make_async_remote_copy(
            src_ref=src, dst_ref=dst, send_sem=send, recv_sem=recv,
            device_id=where, device_id_type=MESH,
        )

    barrier = pltpu.get_barrier_semaphore()

    def greet(k, carry):
        pl.semaphore_signal(barrier, inc=1, device_id={"ctx": lax.rem(me + k, n_ctx)}, device_id_type=MESH)
        return carry

    lax.fori_loop(1, n_ctx, greet, 0)
    for near in x_near:
        pl.semaphore_signal(barrier, inc=1, device_id={"ch": zh * x_n + near}, device_id_type=MESH)
    if zh_n > 1:
        pl.semaphore_signal(barrier, inc=1, device_id={"ch": (1 - zh) * x_n + x}, device_id_type=MESH)

    depth = w_ref.shape[1]
    eye = (lax.broadcasted_iota(jnp.int32, (depth, depth), 0) == lax.broadcasted_iota(jnp.int32, (depth, depth), 1))
    wfull[me] = mm(eye.astype(F32).astype(BF16), w_ref[...], NT).astype(BF16)
    cotfull[mej] = cot_ref[...]
    xt[...] = jnp.transpose(cin_ref[...]).reshape(n_ctx, ROWS, TOK)
    sb[:, chips:] = jnp.zeros((2, lag_blocks, ROWS, TOK), F32)

    pl.semaphore_wait(barrier, (n_ctx - 1) + len(x_near) + (zh_n - 1))

    def w_copy(piece, target):
        return remote(wfull.at[piece], wfull.at[piece], w_send, w_recv.at[piece], ctx=target)

    up = ctx_of(zl, lax.rem(y + 1, y_n), core)
    down = ctx_of(zl, lax.rem(y + y_n - 1, y_n), core)
    half = y_n // 2
    z_of = [lax.rem(zl + k, zl_n) for k in range(zl_n)]

    def goes_up(distance, k):
        return distance < half or (distance == half and k < zl_n // 2)

    def goes_down(distance, k):
        return distance < half or (distance == half and k >= zl_n // 2)

    def w_relay(piece, distance, k, to_up, to_down):
        if to_up and goes_up(distance, k):
            w_copy(piece, up).start()
        if to_down and goes_down(distance, k):
            w_copy(piece, down).start()
        w_copy(piece, sibling).start()

    for k in range(1, zl_n):
        w_copy(me, ctx_of(z_of[k], y, core)).start()
    w_relay(me, 1, 0, y_n > 1, y_n > 1)

    def c_copy(src, plane, xx, rows, sem, near):
        piece = plane * x_n + xx
        return remote(src, cotfull.at[piece, rows], c_send, c_recv.at[piece, sem], ch=plane_target(near))

    def plane_target(near):
        return zh * x_n + near

    everything, low, high = pl.ds(0, TOK), pl.ds(0, TOK // 2), pl.ds(TOK // 2, TOK // 2)

    def c_spread(src, plane):
        for near in x_near:
            c_copy(src.at[everything], plane, x, everything, 0, near).start()

    def c_forward(plane):
        if x_n == 1:
            return
        right, left = x_near
        for source, rows, sem, target in ((left, low, 0, right), (right, high, 1, left)):
            piece = plane * x_n + source
            c_copy(cotfull.at[piece, everything], plane, source, everything, 0, target).wait_recv()
            c_copy(cotfull.at[piece, rows], plane, source, rows, sem, target).start()

    def c_finish(plane):
        if x_n == 1:
            return
        far = lax.rem(x + 2, x_n)
        for rows, sem in ((low, 0), (high, 1)):
            c_copy(cotfull.at[plane * x_n + far, rows], plane, far, rows, sem, far).wait_recv()

    def c_across():
        return remote(cot_ref, cotfull.at[mej], c_send, c_recv.at[mej, 0], ch=(1 - zh) * x_n + x)

    c_spread(cot_ref, zh)
    if zh_n > 1:
        c_across().start()

    def slot_of(target):
        return lax.rem(target, 2) * chips + lax.div(target, 2)

    def x_send(k, carry):
        target = lax.rem(me + k, n_ctx)
        remote(xt.at[slot_of(target)], xb.at[core, chip], x_sem.at[0], x_sem.at[1], ctx=target).start()
        return carry

    lax.fori_loop(1, n_ctx, x_send, 0)
    pltpu.make_async_copy(xt.at[slot_of(me)], xb.at[core, chip], x_sem.at[1]).start()

    for k in range(1, zl_n):
        piece = ctx_of(z_of[k], y, core)
        w_copy(piece, sibling).wait_recv()
        w_relay(piece, 1, k, y_n > 1, y_n > 1)
    c_forward(zh)

    group = core * (chips // 2) + lax.div(chip, 2)
    wide = tap_hi.shape[1]
    row = jnp.pad(filt_ref[pl.ds(group, 1), :], ((0, 0), (0, wide - filt_ref.shape[1])))
    taps = pltpu.roll(jnp.broadcast_to(row, (BLOCK, wide)), 0, 1, stride=1, stride_axis=0)
    tap_hi[...], tap_lo[...] = split(taps)

    def w_step(s):
        for k in range(zl_n):
            if goes_up(s, k):
                piece = ctx_of(z_of[k], lax.rem(y + y_n - s, y_n), core)
                w_copy(piece, sibling).wait_recv()
                w_relay(piece, s + 1, k, True, False)
            if goes_down(s, k):
                piece = ctx_of(z_of[k], lax.rem(y + s, y_n), core)
                w_copy(piece, sibling).wait_recv()
                w_relay(piece, s + 1, k, False, True)

    for s in range(1, half + 1):
        w_step(s)
        if zh_n > 1 and s == max(half - 2, 1):
            other = (1 - zh) * x_n + x
            remote(cotfull.at[other], cotfull.at[other], c_send, c_recv.at[other, 0], ch=mej).wait_recv()
            c_spread(cotfull.at[other], 1 - zh)
    if zh_n > 1:
        if half == 0:
            other = (1 - zh) * x_n + x
            remote(cotfull.at[other], cotfull.at[other], c_send, c_recv.at[other, 0], ch=mej).wait_recv()
            c_spread(cotfull.at[other], 1 - zh)
        c_forward(1 - zh)

    pltpu.make_async_copy(xb, xb, x_sem.at[1]).wait()
    turn = (
        lax.broadcasted_iota(jnp.int32, (BLOCK, BLOCK), 0) + lax.broadcasted_iota(jnp.int32, (BLOCK, BLOCK), 1) == BLOCK - 1
    ).astype(F32).astype(BF16)
    x_all = jnp.concatenate([xb[0].reshape(chips * ROWS, TOK), xb[1].reshape(chips * ROWS, TOK)], axis=1)
    x_hi, x_lo = split(x_all)
    xr_hi[...] = mm(turn, x_hi, NT).astype(BF16)
    xr_lo[...] = mm(turn, x_lo, NT).astype(BF16)

    c_finish(zh)
    if zh_n > 1:
        c_finish(1 - zh)

    def from_sibling(q, carry):
        w_copy(2 * q + 1 - core, sibling).wait_recv()
        return carry

    lax.fori_loop(0, chips, from_sibling, 0)

    per = n_ctx // (zh_n * x_n)
    for j in range(zh_n * x_n):
        term = mm(cotfull[j], wfull[pl.ds(j * per, per)].reshape(per * depth, wfull.shape[2]), NN)
        if j == 0:
            grad[...] = term
        else:
            grad[...] += term
    st[...] = jnp.transpose(grad[...] * gate_ref[...]).reshape(n_ctx, ROWS, TOK)

    def s_send(k, carry):
        target = lax.rem(me + k, n_ctx)
        remote(st.at[slot_of(target)], sb.at[core, chip], s_sem.at[0], s_sem.at[1], ctx=target).start()
        return carry

    lax.fori_loop(1, n_ctx, s_send, 0)
    pltpu.make_async_copy(st.at[slot_of(me)], sb.at[core, chip], s_sem.at[1]).start()
    gg_ref[...] = grad[...] * cout_ref[...]
    arrived = sb.at[:, pl.ds(0, chips)]
    pltpu.make_async_copy(arrived, arrived, s_sem.at[1]).wait()

    total = jnp.zeros((chips * ROWS, BLOCK), F32)
    for d in range(lag_blocks + 1):
        s_rows = jnp.concatenate(
            [sb[0, d : d + chips].reshape(chips * ROWS, TOK), sb[1, d : d + chips].reshape(chips * ROWS, TOK)], axis=1
        )
        s_pair = split(s_rows)
        cols = slice(d * BLOCK, (d + 1) * BLOCK)
        total = total + mm3(s_pair, (tap_hi[:, cols], tap_lo[:, cols]), NT)
        corr[:, cols] = mm3((xr_hi[...], xr_lo[...]), s_pair, NN)
    for c in range(2):
        outt[c] = total[:, c * TOK : (c + 1) * TOK].reshape(chips, ROWS, TOK)

    def o_send(k, carry):
        target = lax.rem(me + k, n_ctx)
        remote(
            outt.at[lax.rem(target, 2), lax.div(target, 2)], rt.at[slot_of(me)], o_sem.at[0], o_sem.at[1], ctx=target
        ).start()
        return carry

    lax.fori_loop(1, n_ctx, o_send, 0)
    pltpu.make_async_copy(outt.at[core, chip], rt.at[slot_of(me)], o_sem.at[1]).start()

    lined = pltpu.roll(corr[...], wide - (BLOCK - 1), 1, stride=1, stride_axis=0)
    lags = jnp.sum(lined, axis=0, keepdims=True) * scale
    for s in range(fgs.shape[0]):
        fgs[s] = lags[:, s * TOK : (s + 1) * TOK]
    place = lax.rem(chip, 2) * chips + core * (chips // 2) + lax.div(chip, 2)
    share = fg_ref.shape[1]

    def f_send(k, carry):
        target = lax.rem(me + k, n_ctx)
        remote(
            fgs.at[lax.div(target * share, TOK)], fgr.at[place], f_sem.at[0], f_sem.at[1], ctx=target
        ).start()
        return carry

    lax.fori_loop(1, n_ctx, f_send, 0)
    pltpu.make_async_copy(fgs.at[lax.div(me * share, TOK)], fgr.at[place], f_sem.at[1]).start()

    pltpu.make_async_copy(rt, rt, o_sem.at[1]).wait()
    ig_ref[...] = jnp.transpose(rt[...].reshape(n_ctx * ROWS, TOK))
    pltpu.make_async_copy(fgr, fgr, f_sem.at[1]).wait()
    parts = fgr[...].reshape(n_ctx, TOK)
    both = parts[:chips] + parts[chips:]
    offset = lax.rem(me * share, TOK)
    fg_ref[...] = pltpu.roll(both, lax.rem(TOK - offset, TOK), 1)[:, :share]

    pltpu.make_async_copy(wfull.at[pl.ds(0, n_ctx - 1)], wfull.at[pl.ds(0, n_ctx - 1)], w_send).wait()
    if zh_n * x_n > 1:
        sent = cotfull.at[pl.ds(0, zh_n * x_n - 1)]
        pltpu.make_async_copy(sent, sent, c_send).wait()
    for ref, sem in ((xt, x_sem), (st, s_sem), (rt, o_sem), (fgr, f_sem)):
        part = ref.at[pl.ds(0, n_ctx - 1)]
        pltpu.make_async_copy(part, part, sem.at[0]).wait()


def shards(grid, cotangent, out_weight, gate_value, conv_output, conv_input, filters):
    tokens, channels = gate_value.shape
    groups, lag_count = filters.shape
    n_ctx, n_ch = lax.axis_size("ctx"), lax.axis_size("ch")
    chips = n_ctx // 2
    lag_blocks = -(-lag_count // BLOCK)
    wide = (lag_blocks + 1) * BLOCK
    segments = -(-lag_count // TOK)
    scale = 1.0 / math.sqrt(channels // groups * tokens * n_ctx)
    dims = (grid["z_lo"], grid["y"], grid["z_hi"], grid["x"], lag_blocks)
    vmem = pl.BlockSpec(memory_space=pltpu.VMEM)
    dma = pltpu.SemaphoreType.DMA
    return pl.pallas_call(
        functools.partial(kernel, dims, scale),
        out_shape=(
            jax.ShapeDtypeStruct((tokens, channels), F32),
            jax.ShapeDtypeStruct((tokens, channels), F32),
            jax.ShapeDtypeStruct((groups, lag_count // n_ctx), F32),
        ),
        in_specs=[vmem] * 6,
        out_specs=(vmem,) * 3,
        scratch_shapes=[
            pltpu.VMEM((n_ctx, out_weight.shape[1], channels), BF16),
            pltpu.VMEM((n_ch, tokens, channels), BF16),
            pltpu.VMEM((n_ctx, ROWS, TOK), F32),
            pltpu.VMEM((2, chips, ROWS, TOK), F32),
            pltpu.VMEM((n_ctx, ROWS, TOK), F32),
            pltpu.VMEM((2, chips + lag_blocks, ROWS, TOK), F32),
            pltpu.VMEM((2, chips, ROWS, TOK), F32),
            pltpu.VMEM((n_ctx, ROWS, TOK), F32),
            pltpu.VMEM((BLOCK, wide), BF16),
            pltpu.VMEM((BLOCK, wide), BF16),
            pltpu.VMEM((BLOCK, chips * ROWS), BF16),
            pltpu.VMEM((BLOCK, chips * ROWS), BF16),
            pltpu.VMEM((BLOCK, wide), F32),
            pltpu.VMEM((segments, 1, TOK), F32),
            pltpu.VMEM((n_ctx, 1, TOK), F32),
            pltpu.VMEM((tokens, channels), F32),
            dma,
            dma((n_ctx,)),
            dma,
            dma((n_ch, 2)),
            dma((2,)),
            dma((2,)),
            dma((2,)),
            dma((2,)),
        ],
        compiler_params=pltpu.CompilerParams(
            collective_id=0, has_side_effects=True, vmem_limit_bytes=48 * 1024 * 1024
        ),
    )(cotangent, out_weight, gate_value, conv_output, conv_input, filters)


def solution(mesh, grid=GRID):
    return jax.shard_map(
        functools.partial(shards, grid),
        mesh=mesh,
        in_specs=(
            P("ctx", "ch"),
            P("ch", "ctx"),
            P("ctx", "ch"),
            P("ctx", "ch"),
            P("ctx", "ch"),
            P("ch", None),
        ),
        out_specs=(P("ctx", "ch"), P("ctx", "ch"), P("ch", "ctx")),
        check_vma=False,
    )
```

time: 711 us -> 89.2 us (0.13)
  waiting for transfers between devices: 537 us -> 0 us
  Pallas kernels: 0 us -> 81.4 us
  loops' own time: 33.8 us -> 0 us
  local copies, waits for them, and re-layouts: 39.4 us -> 6.8 us
  starting transfers between devices: 30.9 us -> 0 us
  matrix products: 27.7 us -> 0 us
  other arithmetic: 22.5 us -> 0 us
  between operations: 13.9 us -> 0.67 us
    unnamed x4 -> x0, waiting for transfers between devices: 309 us -> none
    all_gather x2 -> x0, waiting for transfers between devices: 189 us -> none  [the longest x1 120 us: shards(): lax.all_gather(out_weight, 'ctx', axis=1, tiled=True)]
    pallas_call x0 -> x1, Pallas kernels: none -> 81.4 us  [shards(): pl.pallas_call(functools.partial(kernel, dims, scale), out_shape=(jax.Sha...]
    ppermute x16 -> x0, waiting for transfers between devices: 38.8 us -> none  [shifted(): return lax.ppermute(block, axis, route)]
    another operation x1 -> x0, loops' own time: 33.8 us -> none  [shards(): lax.scan(relay_step, (seq_grad, spectra), jnp.arange(1, ahead_blocks + 1,...]
    ppermute x16 -> x0, starting transfers between devices: 30.8 us -> none  [shifted(): return lax.ppermute(block, axis, route)]
    dot_general x22 -> x0, matrix products: 27.7 us -> none  [the longest x17 17.4 us: spectrum_step(): block_spectrum = jnp.dot(forward_rows, shard_block, precision=exact_mode)]
    mul x17 -> x0, local copies, waits for them, and re-layouts: 12.6 us -> none  [spectrum_step(): prod_real = block_real * filter_real + block_imag * filter_imag]
  transfers between devices with their start and end apart: 19 -> 0, of which waited for: 19 -> 0; matrix products, arithmetic and copies ran while one was open for 4% -> 0% of each run, Pallas kernels for 0% -> 0%
where the time goes in v1:
time: 89.2 us; the launch traced here: 88.9 us
  Pallas kernels  81.4 us (91%)
  local copies, waits for them, and re-layouts  6.8 us (8%)
    pallas_call x1, Pallas kernels, shards(): pl.pallas_call(functools.partial(kernel, dims, scale), out_shape=(jax.Sha...  81.4 us
    unnamed x14, local copies, waits for them, and re-layouts  6.8 us

profile of v1, /device:TPU:1, one launch (start us, length us, event | category | flops | bytes accessed | tf_op | source)
XLA Modules:
  0.0 88.9 jit_solution(4694583895997075381)
XLA Ops:
  0.6 0.0 copy-start.4
  0.6 1.0 %copy.9.w_ref = bf16[512,64]{1,0:T(8,128)(2,1)S(1)} copy(bf16[512,64]{0,1:T(8,128)(2,1)} %param.7) | data formatting | bytes 131072 | tf_op args[1]
  1.6 0.0 copy-done.4
  1.6 0.0 copy-start
  1.7 0.9 %copy-done = f32[128,512]{1,0:T(8,128)S(1)} copy-done((f32[128,512]{1,0:T(8,128)S(1)}, f32[128,512]{1,0:T(8,128)}, u32[]{:S(2)}) %copy-start) | copy-done | bytes 262168
  2.6 0.0 copy-start.1
  2.6 0.9 %copy-done.1 = f32[128,512]{1,0:T(8,128)S(1)} copy-done((f32[128,512]{1,0:T(8,128)S(1)}, f32[128,512]{1,0:T(8,128)}, u32[]{:S(2)}) %copy-start.1) | copy-done | bytes 262168
  3.6 0.0 copy-start.2
  3.6 0.9 %copy-done.2 = f32[128,512]{1,0:T(8,128)S(1)} copy-done((f32[128,512]{1,0:T(8,128)S(1)}, f32[128,512]{1,0:T(8,128)}, u32[]{:S(2)}) %copy-start.2) | copy-done | bytes 262168
  4.5 0.0 copy-start.3
  4.5 0.9 %copy-done.3 = f32[32,2048]{1,0:T(8,128)S(1)} copy-done((f32[32,2048]{1,0:T(8,128)S(1)}, f32[32,2048]{1,0:T(8,128)}, u32[]{:S(2)}) %copy-start.3) | copy-done | bytes 262168
  5.5 81.4 %shard_map.85 = (f32[128,512]{1,0:T(8,128)S(1)}, f32[128,512]{1,0:T(8,128)S(1)}, f32[32,32]{1,0:T(8,128)S(1)}) custom-call(bf16[128,512]{1,0:T(8,128)(2,1)S(1)} %copy-done.4, bf16[512,64]{1,0:T(8,128)(2,1)S(1)} %copy.9.w_ref, f32[128,512]{1,0:T(8,128)S(1)} %copy-done, f32[128,512]{1,0:T(8,128)S(1)} %copy-done.1, f32[128,512]{1,0:T(8,128)S(1)} %copy-done.2, ...), custom_call_target="tpu_custom_call" | custom-call | tf_op jit(solution)/shard_map/pallas_call | solution.py:300
  86.9 0.7 copy.13
  87.6 0.7 copy.14
  88.3 0.6 copy.15
Async XLA Ops:
  0.6 1.0 %copy-start.4 = (bf16[128,512]{1,0:T(8,128)(2,1)S(1)}, bf16[128,512]{1,0:T(8,128)(2,1)}, u32[]{:S(2)}) copy-start(bf16[128,512]{1,0:T(8,128)(2,1)} %cot_ref.1) | copy-start | bytes 393220
  1.6 1.0 %copy-start = (f32[128,512]{1,0:T(8,128)S(1)}, f32[128,512]{1,0:T(8,128)}, u32[]{:S(2)}) copy-start(f32[128,512]{1,0:T(8,128)} %gate_ref.1) | copy-start | bytes 786436
  2.6 0.9 %copy-start.1 = (f32[128,512]{1,0:T(8,128)S(1)}, f32[128,512]{1,0:T(8,128)}, u32[]{:S(2)}) copy-start(f32[128,512]{1,0:T(8,128)} %cout_ref.1) | copy-start | bytes 786436
  3.6 0.9 %copy-start.2 = (f32[128,512]{1,0:T(8,128)S(1)}, f32[128,512]{1,0:T(8,128)}, u32[]{:S(2)}) copy-start(f32[128,512]{1,0:T(8,128)} %cin_ref.1) | copy-start | bytes 786436
  4.5 0.9 %copy-start.3 = (f32[32,2048]{1,0:T(8,128)S(1)}, f32[32,2048]{1,0:T(8,128)}, u32[]{:S(2)}) copy-start(f32[32,2048]{1,0:T(8,128)} %filt_ref.1) | copy-start | bytes 786436

commit v2 on v1

v2 whole, which is shorter than its diff:
```python
import functools
import math

import jax
import jax.numpy as jnp
from jax import lax
from jax.experimental import pallas as pl
from jax.experimental.pallas import tpu as pltpu
from jax.sharding import PartitionSpec as P

MESH = pl.DeviceIdType.MESH
F32, BF16 = jnp.float32, jnp.bfloat16
NT = (((1,), (1,)), ((), ()))
NN = (((1,), (0,)), ((), ()))
GRID = {"z_lo": 4, "y": 8, "z_hi": 2, "x": 4}
TOK = 128
BLOCK = 2 * TOK
ROWS = 8


def split(value):
    high = value.astype(BF16)
    return high, (value - high.astype(F32)).astype(BF16)


def mm(a, b, dims):
    return lax.dot_general(a, b, dims, preferred_element_type=F32)


def mm3(a, b, dims):
    return mm(a[0], b[0], dims) + (mm(a[0], b[1], dims) + mm(a[1], b[0], dims))


def kernel(
    dims, scale,
    cot_hbm, w_hbm, gate_hbm, cout_hbm, cin_hbm, filt_hbm,
    ig_ref, gg_ref, fg_ref,
    gate_ref, cout_ref, cin_ref, filt_ref, wfull, cotfull, xt, xb, st, sb, outt, rt, tap_hi, tap_lo, xr_hi, xr_lo, corr, fgs, fgr, grad,
    w_send, w_recv, c_send, c_recv, x_sem, s_sem, o_sem, f_sem, in_sem,
):
    zl_n, y_n, zh_n, x_n, lag_blocks = dims
    chips = zl_n * y_n
    n_ctx = 2 * chips
    me = lax.axis_index("ctx")
    core = lax.rem(me, 2)
    chip = lax.div(me, 2)
    y = lax.rem(chip, y_n)
    zl = lax.div(chip, y_n)
    mej = lax.axis_index("ch")
    x = lax.rem(mej, x_n)
    zh = lax.div(mej, x_n)
    sibling = me + 1 - 2 * core
    x_far = [lax.rem(x + k, x_n) for k in (1, 3, 2) if k < x_n]

    def ctx_of(z_, y_, c_):
        return (z_ * y_n + y_) * 2 + c_

    def remote(src, dst, send, recv, **where):
        return pltpu.make_async_remote_copy(
            src_ref=src, dst_ref=dst, send_sem=send, recv_sem=recv,
            device_id=where, device_id_type=MESH,
        )

    def everyone(send):
        for dy in sorted(range(y_n), key=lambda k: -min(k, y_n - k)):
            for dz in range(zl_n):
                for other in (True, False):
                    if dy or dz or other:
                        c_ = 1 - core if other else core
                        chip_ = z_of[dz] * y_n + y_of[dy]
                        send(2 * chip_ + c_, c_, chip_, c_ * chips + chip_)

    home = core * chips + chip

    barrier = pltpu.get_barrier_semaphore()

    half = y_n // 2
    z_of = [lax.rem(zl + k, zl_n) for k in range(zl_n)]
    y_of = [lax.rem(y + k, y_n) for k in range(y_n)]
    up, down = (ctx_of(zl, y_of[k % y_n], core) for k in (1, y_n - 1))
    rings = [sibling] + ([up, down] if y_n > 2 else [up] * (y_n > 1)) + [ctx_of(z, y, core) for z in z_of[1:]]
    for near in rings:
        pl.semaphore_signal(barrier, inc=1, device_id={"ctx": near}, device_id_type=MESH)
    for near in x_far:
        pl.semaphore_signal(barrier, inc=1, device_id={"ch": zh * x_n + near}, device_id_type=MESH)
    if zh_n > 1:
        pl.semaphore_signal(barrier, inc=1, device_id={"ch": (1 - zh) * x_n + x}, device_id_type=MESH)

    group = core * (chips // 2) + lax.div(chip, 2)
    some = filt_ref.shape[0]
    loads = [
        pltpu.make_async_copy(src, dst, in_sem.at[n])
        for n, (src, dst) in enumerate(
            (
                (cin_hbm, cin_ref),
                (w_hbm, wfull.at[me]),
                (cot_hbm, cotfull.at[mej]),
                (filt_hbm.at[pl.ds(lax.div(group, some) * some, some)], filt_ref),
                (gate_hbm, gate_ref),
                (cout_hbm, cout_ref),
            )
        )
    ]
    for load in loads:
        load.start()
    sb[:, chips:] = jnp.zeros((2, lag_blocks, ROWS, TOK), F32)
    loads[0].wait()
    xt[...] = jnp.transpose(cin_ref[...]).reshape(n_ctx, ROWS, TOK)
    loads[1].wait()
    loads[2].wait()
    depth = w_hbm.shape[0]

    pl.semaphore_wait(barrier, len(rings) + len(x_far) + (zh_n - 1))

    def w_copy(piece, target):
        return remote(wfull.at[piece], wfull.at[piece], w_send, w_recv.at[piece], ctx=target)

    def goes_up(distance, k):
        return distance < half or (distance == half and k < zl_n // 2)

    def goes_down(distance, k):
        return distance < half or (distance == half and k >= zl_n // 2)

    def w_relay(piece, distance, k, to_up, to_down):
        if to_up and goes_up(distance, k):
            w_copy(piece, up).start()
        if to_down and goes_down(distance, k):
            w_copy(piece, down).start()
        w_copy(piece, sibling).start()

    for k in range(1, zl_n):
        w_copy(me, ctx_of(z_of[k], y, core)).start()
    w_relay(me, 1, 0, y_n > 1, y_n > 1)

    def c_copy(piece, xx):
        return remote(cotfull.at[piece], cotfull.at[piece], c_send, c_recv.at[piece], ch=zh * x_n + xx)

    def c_spread(piece):
        for xx in x_far:
            c_copy(piece, xx).start()

    across = (1 - zh) * x_n + x
    if zh_n > 1:
        remote(cotfull.at[mej], cotfull.at[mej], c_send, c_recv.at[mej], ch=across).start()
    c_spread(mej)

    loads[3].wait()
    wide = tap_hi.shape[1]
    row = jnp.pad(filt_ref[pl.ds(lax.rem(group, some), 1), :], ((0, 0), (0, wide - filt_ref.shape[1])))
    taps = pltpu.roll(jnp.broadcast_to(row, (BLOCK, wide)), 0, 1, stride=1, stride_axis=0)
    tap_hi[...], tap_lo[...] = split(taps)

    def from_z(k):
        piece = ctx_of(z_of[k], y, core)
        w_copy(piece, sibling).wait_recv()
        w_relay(piece, 1, k, y_n > 1, y_n > 1)

    def from_y(s, k):
        if goes_up(s, k):
            piece = ctx_of(z_of[k], y_of[y_n - s], core)
            w_copy(piece, sibling).wait_recv()
            w_relay(piece, s + 1, k, True, False)
        if goes_down(s, k):
            piece = ctx_of(z_of[k], y_of[s], core)
            w_copy(piece, sibling).wait_recv()
            w_relay(piece, s + 1, k, False, True)

    if half:
        from_y(1, 0)
    for k in range(1, zl_n):
        from_z(k)
    for s in range(1, half + 1):
        if s < half:
            from_y(s + 1, 0)
        for k in range(1, zl_n):
            from_y(s, k)
        if zh_n > 1 and s == min(2, half):
            c_copy(across, x).wait_recv()
            c_spread(across)
    for piece in range(zh_n * x_n):
        first = lax.rem(mej + piece, zh_n * x_n)
        if piece and zh_n > 1:
            @pl.when(first != across)
            def _():
                c_copy(first, x).wait_recv()
        elif piece:
            c_copy(first, x).wait_recv()

    def from_sibling(q, carry):
        w_copy(2 * q + 1 - core, sibling).wait_recv()
        return carry

    lax.fori_loop(0, chips, from_sibling, 0)

    per = n_ctx // (zh_n * x_n)
    for j in range(zh_n * x_n):
        term = mm(cotfull[j], wfull[pl.ds(j * per, per)].reshape(per * depth, wfull.shape[2]), NN)
        if j == 0:
            grad[...] = term
        else:
            grad[...] += term
    loads[4].wait()
    st[...] = jnp.transpose(grad[...] * gate_ref[...]).reshape(n_ctx, ROWS, TOK)

    def s_send(target, c_, chip_, slot):
        remote(st.at[slot], sb.at[core, chip], s_sem.at[0], s_sem.at[1], ctx=target).start()

    everyone(s_send)
    pltpu.make_async_copy(st.at[home], sb.at[core, chip], s_sem.at[1]).start()

    def x_send(target, c_, chip_, slot):
        remote(xt.at[slot], xb.at[core, chip], x_sem.at[0], x_sem.at[1], ctx=target).start()

    everyone(x_send)
    pltpu.make_async_copy(xt.at[home], xb.at[core, chip], x_sem.at[1]).start()
    loads[5].wait()
    gg_ref[...] = grad[...] * cout_ref[...]
    arrived = sb.at[:, pl.ds(0, chips)]
    pltpu.make_async_copy(arrived, arrived, s_sem.at[1]).wait()

    def s_rows(d):
        return split(jnp.concatenate(
            [sb[0, d : d + chips].reshape(chips * ROWS, TOK), sb[1, d : d + chips].reshape(chips * ROWS, TOK)], axis=1
        ))

    blocks = [slice(d * BLOCK, (d + 1) * BLOCK) for d in range(lag_blocks + 1)]
    total = jnp.zeros((chips * ROWS, BLOCK), F32)
    for d, cols in enumerate(blocks):
        total = total + mm3(s_rows(d), (tap_hi[:, cols], tap_lo[:, cols]), NT)
    for c in range(2):
        outt[c] = total[:, c * TOK : (c + 1) * TOK].reshape(chips, ROWS, TOK)

    def o_send(target, c_, chip_, slot):
        remote(outt.at[c_, chip_], rt.at[home], o_sem.at[0], o_sem.at[1], ctx=target).start()

    everyone(o_send)
    pltpu.make_async_copy(outt.at[core, chip], rt.at[home], o_sem.at[1]).start()

    pltpu.make_async_copy(xb, xb, x_sem.at[1]).wait()
    turn = (
        lax.broadcasted_iota(jnp.int32, (BLOCK, BLOCK), 0) + lax.broadcasted_iota(jnp.int32, (BLOCK, BLOCK), 1) == BLOCK - 1
    ).astype(F32).astype(BF16)
    x_all = jnp.concatenate([xb[0].reshape(chips * ROWS, TOK), xb[1].reshape(chips * ROWS, TOK)], axis=1)
    x_hi, x_lo = split(x_all)
    xr_hi[...] = mm(turn, x_hi, NT).astype(BF16)
    xr_lo[...] = mm(turn, x_lo, NT).astype(BF16)

    for d, cols in enumerate(blocks):
        corr[:, cols] = mm3((xr_hi[...], xr_lo[...]), s_rows(d), NN)

    lined = pltpu.roll(corr[...], wide - (BLOCK - 1), 1, stride=1, stride_axis=0)
    lags = jnp.sum(lined, axis=0, keepdims=True) * scale
    for s in range(fgs.shape[0]):
        fgs[s] = lags[:, s * TOK : (s + 1) * TOK]
    place = lax.rem(chip, 2) * chips + core * (chips // 2) + lax.div(chip, 2)
    share = fg_ref.shape[1]

    def f_send(target, c_, chip_, slot):
        remote(fgs.at[lax.div(chip_ * (2 * share), TOK)], fgr.at[place], f_sem.at[0], f_sem.at[1], ctx=target).start()

    everyone(f_send)
    pltpu.make_async_copy(fgs.at[lax.div(chip * (2 * share), TOK)], fgr.at[place], f_sem.at[1]).start()

    pltpu.make_async_copy(rt, rt, o_sem.at[1]).wait()
    ig_ref[...] = jnp.transpose(rt[...].reshape(n_ctx * ROWS, TOK))
    pltpu.make_async_copy(fgr, fgr, f_sem.at[1]).wait()
    parts = fgr[...].reshape(n_ctx, TOK)
    both = parts[:chips] + parts[chips:]
    offset = lax.rem(me * share, TOK)
    fg_ref[...] = pltpu.roll(both, lax.rem(TOK - offset, TOK), 1)[:, :share]

    pltpu.make_async_copy(wfull.at[pl.ds(0, n_ctx - 1)], wfull.at[pl.ds(0, n_ctx - 1)], w_send).wait()
    if zh_n * x_n > 1:
        sent = cotfull.at[pl.ds(0, zh_n * x_n - 1)]
        pltpu.make_async_copy(sent, sent, c_send).wait()
    for ref, sem in ((xt, x_sem), (st, s_sem), (rt, o_sem), (fgr, f_sem)):
        part = ref.at[pl.ds(0, n_ctx - 1)]
        pltpu.make_async_copy(part, part, sem.at[0]).wait()


def shards(grid, cotangent, out_weight, gate_value, conv_output, conv_input, filters):
    tokens, channels = gate_value.shape
    groups, lag_count = filters.shape
    n_ctx, n_ch = lax.axis_size("ctx"), lax.axis_size("ch")
    chips = n_ctx // 2
    lag_blocks = -(-lag_count // BLOCK)
    wide = (lag_blocks + 1) * BLOCK
    segments = -(-lag_count // TOK)
    scale = 1.0 / math.sqrt(channels // groups * tokens * n_ctx)
    dims = (grid["z_lo"], grid["y"], grid["z_hi"], grid["x"], lag_blocks)
    vmem = pl.BlockSpec(memory_space=pltpu.VMEM)
    dma = pltpu.SemaphoreType.DMA
    return pl.pallas_call(
        functools.partial(kernel, dims, scale),
        out_shape=(
            jax.ShapeDtypeStruct((tokens, channels), F32),
            jax.ShapeDtypeStruct((tokens, channels), F32),
            jax.ShapeDtypeStruct((groups, lag_count // n_ctx), F32),
        ),
        in_specs=[pl.BlockSpec(memory_space=pltpu.HBM)] * 6,
        out_specs=(vmem,) * 3,
        scratch_shapes=[
            pltpu.VMEM((tokens, channels), F32),
            pltpu.VMEM((tokens, channels), F32),
            pltpu.VMEM((tokens, channels), F32),
            pltpu.VMEM((min(8, groups), lag_count), F32),
            pltpu.VMEM((n_ctx, out_weight.shape[1], channels), BF16),
            pltpu.VMEM((n_ch, tokens, channels), BF16),
            pltpu.VMEM((n_ctx, ROWS, TOK), F32),
            pltpu.VMEM((2, chips, ROWS, TOK), F32),
            pltpu.VMEM((n_ctx, ROWS, TOK), F32),
            pltpu.VMEM((2, chips + lag_blocks, ROWS, TOK), F32),
            pltpu.VMEM((2, chips, ROWS, TOK), F32),
            pltpu.VMEM((n_ctx, ROWS, TOK), F32),
            pltpu.VMEM((BLOCK, wide), BF16),
            pltpu.VMEM((BLOCK, wide), BF16),
            pltpu.VMEM((BLOCK, chips * ROWS), BF16),
            pltpu.VMEM((BLOCK, chips * ROWS), BF16),
            pltpu.VMEM((BLOCK, wide), F32),
            pltpu.VMEM((segments, 1, TOK), F32),
            pltpu.VMEM((n_ctx, 1, TOK), F32),
            pltpu.VMEM((tokens, channels), F32),
            dma,
            dma((n_ctx,)),
            dma,
            dma((n_ch,)),
            dma((2,)),
            dma((2,)),
            dma((2,)),
            dma((2,)),
            dma((6,)),
        ],
        compiler_params=pltpu.CompilerParams(
            collective_id=0, has_side_effects=True, vmem_limit_bytes=66_000_000
        ),
    )(cotangent, out_weight.T, gate_value, conv_output, conv_input, filters)


def solution(mesh, grid=GRID):
    return jax.shard_map(
        functools.partial(shards, grid),
        mesh=mesh,
        in_specs=(
            P("ctx", "ch"),
            P("ch", "ctx"),
            P("ctx", "ch"),
            P("ctx", "ch"),
            P("ctx", "ch"),
            P("ch", None),
        ),
        out_specs=(P("ctx", "ch"), P("ctx", "ch"), P("ch", "ctx")),
        check_vma=False,
    )
```

time: 89.2 us -> 75.8 us (0.85)
  Pallas kernels: 81.4 us -> 71.9 us
  local copies, waits for them, and re-layouts: 6.8 us -> 3.04 us
    pallas_call x1, Pallas kernels: 81.4 us -> 71.9 us  [shards(): pl.pallas_call(functools.partial(kernel, dims, scale), out_shape=(jax.Sha...]
    unnamed x14 -> x7, local copies, waits for them, and re-layouts: 6.8 us -> 3.04 us
where the time goes in v2:
time: 75.8 us; the launch traced here: 75.6 us
  Pallas kernels  71.9 us (95%)
  local copies, waits for them, and re-layouts  3.04 us (4%)
    pallas_call x1, Pallas kernels, shards(): pl.pallas_call(functools.partial(kernel, dims, scale), out_shape=(jax.Sha...  71.9 us
    unnamed x7, local copies, waits for them, and re-layouts  3.04 us

profile of v2, /device:TPU:1, one launch (start us, length us, event | category | flops | bytes accessed | tf_op | source)
XLA Modules:
  0.0 75.6 jit_solution(8609226706834981308)
XLA Ops:
  0.6 71.9 %shard_map.85 = (f32[128,512]{1,0:T(8,128)}, f32[128,512]{1,0:T(8,128)}, f32[32,32]{1,0:T(8,128)}) custom-call(bf16[128,512]{1,0:T(8,128)(2,1)} %cot_hbm.1, bf16[64,512]{1,0:T(8,128)(2,1)} %bitcast.1, f32[128,512]{1,0:T(8,128)} %gate_hbm.1, f32[128,512]{1,0:T(8,128)} %cout_hbm.1, f32[128,512]{1,0:T(8,128)} %cin_hbm.1, f32[32,2048]{1,0:T(8,128)} %filt_hbm.1), custom_call_target="tpu_custom_call" | custom-call | tf_op jit(solution)/shard_map/pallas_call | solution.py:293
  72.5 0.0 copy-start
  72.6 1.7 %copy.12 = f32[128,512]{1,0:T(8,128)} copy(f32[128,512]{1,0:T(8,128)} %get-tuple-element.6) | data formatting | bytes 524288
  74.3 0.0 copy-done
  74.3 0.0 copy-start.1
  74.3 0.7 copy.13
  75.0 0.0 copy-done.1
  75.0 0.6 copy.14
Async XLA Ops:
  72.5 1.7 %copy-start = (f32[128,512]{1,0:T(8,128)S(1)}, f32[128,512]{1,0:T(8,128)}, u32[]{:S(2)}) copy-start(f32[128,512]{1,0:T(8,128)} %get-tuple-element.7) | copy-start | bytes 786436
  74.3 0.7 copy-start.1

commit v3 on v2

--- a/solution.py
+++ b/solution.py
@@ -104,8 +104,6 @@
     for load in loads:
         load.start()
     sb[:, chips:] = jnp.zeros((2, lag_blocks, ROWS, TOK), F32)
-    loads[0].wait()
-    xt[...] = jnp.transpose(cin_ref[...]).reshape(n_ctx, ROWS, TOK)
     loads[1].wait()
     loads[2].wait()
     depth = w_hbm.shape[0]
@@ -140,15 +138,7 @@
             c_copy(piece, xx).start()
 
     across = (1 - zh) * x_n + x
-    if zh_n > 1:
-        remote(cotfull.at[mej], cotfull.at[mej], c_send, c_recv.at[mej], ch=across).start()
     c_spread(mej)
-
-    loads[3].wait()
-    wide = tap_hi.shape[1]
-    row = jnp.pad(filt_ref[pl.ds(lax.rem(group, some), 1), :], ((0, 0), (0, wide - filt_ref.shape[1])))
-    taps = pltpu.roll(jnp.broadcast_to(row, (BLOCK, wide)), 0, 1, stride=1, stride_axis=0)
-    tap_hi[...], tap_lo[...] = split(taps)
 
     def from_z(k):
         piece = ctx_of(z_of[k], y, core)
@@ -169,12 +159,22 @@
         from_y(1, 0)
     for k in range(1, zl_n):
         from_z(k)
+    if zh_n > 1:
+        remote(cotfull.at[mej], cotfull.at[mej], c_send, c_recv.at[mej], ch=across).start()
+    loads[3].wait()
+    wide = tap_hi.shape[1]
+    row = jnp.pad(filt_ref[pl.ds(lax.rem(group, some), 1), :], ((0, 0), (0, wide - filt_ref.shape[1])))
+    taps = pltpu.roll(jnp.broadcast_to(row, (BLOCK, wide)), 0, 1, stride=1, stride_axis=0)
+    tap_hi[...], tap_lo[...] = split(taps)
+
+    loads[0].wait()
+    xt[...] = jnp.transpose(cin_ref[...]).reshape(n_ctx, ROWS, TOK)
     for s in range(1, half + 1):
         if s < half:
             from_y(s + 1, 0)
         for k in range(1, zl_n):
             from_y(s, k)
-        if zh_n > 1 and s == min(2, half):
+        if zh_n > 1 and s == 1:
             c_copy(across, x).wait_recv()
             c_spread(across)
     for piece in range(zh_n * x_n):

time: 75.8 us -> 71.4 us (0.942)
  Pallas kernels: 71.9 us -> 67.5 us
    pallas_call x1, Pallas kernels: 71.9 us -> 67.5 us  [shards(): pl.pallas_call(functools.partial(kernel, dims, scale), out_shape=(jax.Sha...]
where the time goes in v3:
time: 71.4 us; the launch traced here: 71.2 us
  Pallas kernels  67.5 us (95%)
  local copies, waits for them, and re-layouts  3.04 us (4%)
    pallas_call x1, Pallas kernels, shards(): pl.pallas_call(functools.partial(kernel, dims, scale), out_shape=(jax.Sha...  67.5 us
    unnamed x7, local copies, waits for them, and re-layouts  3.04 us

profile of v3, /device:TPU:1, one launch (start us, length us, event | category | flops | bytes accessed | tf_op | source)
XLA Modules:
  0.0 71.2 jit_solution(7174566577001735568)
XLA Ops:
  0.6 67.5 %shard_map.85 = (f32[128,512]{1,0:T(8,128)}, f32[128,512]{1,0:T(8,128)}, f32[32,32]{1,0:T(8,128)}) custom-call(bf16[128,512]{1,0:T(8,128)(2,1)} %cot_hbm.1, bf16[64,512]{1,0:T(8,128)(2,1)} %bitcast.1, f32[128,512]{1,0:T(8,128)} %gate_hbm.1, f32[128,512]{1,0:T(8,128)} %cout_hbm.1, f32[128,512]{1,0:T(8,128)} %cin_hbm.1, f32[32,2048]{1,0:T(8,128)} %filt_hbm.1), custom_call_target="tpu_custom_call" | custom-call | tf_op jit(solution)/shard_map/pallas_call | solution.py:293
  68.2 0.0 copy-start
  68.2 1.7 %copy.12 = f32[128,512]{1,0:T(8,128)} copy(f32[128,512]{1,0:T(8,128)} %get-tuple-element.6) | data formatting | bytes 524288
  69.9 0.0 copy-done
  69.9 0.0 copy-start.1
  69.9 0.7 copy.13
  70.6 0.0 copy-done.1
  70.6 0.6 copy.14
Async XLA Ops:
  68.2 1.7 %copy-start = (f32[128,512]{1,0:T(8,128)S(1)}, f32[128,512]{1,0:T(8,128)}, u32[]{:S(2)}) copy-start(f32[128,512]{1,0:T(8,128)} %get-tuple-element.7) | copy-start | bytes 786436
  69.9 0.7 %copy-start.1 = (f32[32,32]{1,0:T(8,128)S(1)}, f32[32,32]{1,0:T(8,128)}, u32[]{:S(2)}) copy-start(f32[32,32]{1,0:T(8,128)} %get-tuple-element.8) | copy-start | bytes 12292

commit v4 on v3

--- a/solution.py
+++ b/solution.py
@@ -34,8 +34,8 @@
 def kernel(
     dims, scale,
     cot_hbm, w_hbm, gate_hbm, cout_hbm, cin_hbm, filt_hbm,
-    ig_ref, gg_ref, fg_ref,
-    gate_ref, cout_ref, cin_ref, filt_ref, wfull, cotfull, xt, xb, st, sb, outt, rt, tap_hi, tap_lo, xr_hi, xr_lo, corr, fgs, fgr, grad,
+    rt, gg_hbm, fgr,
+    gate_ref, cout_ref, cin_ref, filt_ref, wfull, cotfull, gg_ref, xt, xb, st, sb, outt, tap_hi, tap_lo, xr_hi, xr_lo, corr, fgs, grad,
     w_send, w_recv, c_send, c_recv, x_sem, s_sem, o_sem, f_sem, in_sem,
 ):
     zl_n, y_n, zh_n, x_n, lag_blocks = dims
@@ -215,6 +215,8 @@
     pltpu.make_async_copy(xt.at[home], xb.at[core, chip], x_sem.at[1]).start()
     loads[5].wait()
     gg_ref[...] = grad[...] * cout_ref[...]
+    gate_out = pltpu.make_async_copy(gg_ref, gg_hbm, in_sem.at[0])
+    gate_out.start()
     arrived = sb.at[:, pl.ds(0, chips)]
     pltpu.make_async_copy(arrived, arrived, s_sem.at[1]).wait()
 
@@ -253,7 +255,7 @@
     for s in range(fgs.shape[0]):
         fgs[s] = lags[:, s * TOK : (s + 1) * TOK]
     place = lax.rem(chip, 2) * chips + core * (chips // 2) + lax.div(chip, 2)
-    share = fg_ref.shape[1]
+    share = filt_hbm.shape[1] // n_ctx
 
     def f_send(target, c_, chip_, slot):
         remote(fgs.at[lax.div(chip_ * (2 * share), TOK)], fgr.at[place], f_sem.at[0], f_sem.at[1], ctx=target).start()
@@ -261,13 +263,9 @@
     everyone(f_send)
     pltpu.make_async_copy(fgs.at[lax.div(chip * (2 * share), TOK)], fgr.at[place], f_sem.at[1]).start()
 
+    gate_out.wait()
     pltpu.make_async_copy(rt, rt, o_sem.at[1]).wait()
-    ig_ref[...] = jnp.transpose(rt[...].reshape(n_ctx * ROWS, TOK))
     pltpu.make_async_copy(fgr, fgr, f_sem.at[1]).wait()
-    parts = fgr[...].reshape(n_ctx, TOK)
-    both = parts[:chips] + parts[chips:]
-    offset = lax.rem(me * share, TOK)
-    fg_ref[...] = pltpu.roll(both, lax.rem(TOK - offset, TOK), 1)[:, :share]
 
     pltpu.make_async_copy(wfull.at[pl.ds(0, n_ctx - 1)], wfull.at[pl.ds(0, n_ctx - 1)], w_send).wait()
     if zh_n * x_n > 1:
@@ -276,6 +274,17 @@
     for ref, sem in ((xt, x_sem), (st, s_sem), (rt, o_sem), (fgr, f_sem)):
         part = ref.at[pl.ds(0, n_ctx - 1)]
         pltpu.make_async_copy(part, part, sem.at[0]).wait()
+
+
+def finish(rt, gg_in, fgr, ig_ref, gg_ref, fg_ref):
+    n_ctx = fgr.shape[0]
+    ig_ref[...] = jnp.transpose(rt[...].reshape(n_ctx * ROWS, TOK))
+    gg_ref[...] = gg_in[...]
+    parts = fgr[...].reshape(n_ctx, TOK)
+    both = parts[: n_ctx // 2] + parts[n_ctx // 2 :]
+    share = fg_ref.shape[1]
+    offset = lax.rem(lax.axis_index("ctx") * share, TOK)
+    fg_ref[...] = pltpu.roll(both, lax.rem(TOK - offset, TOK), 1)[:, :share]
 
 
 def shards(grid, cotangent, out_weight, gate_value, conv_output, conv_input, filters):
@@ -290,15 +299,16 @@
     dims = (grid["z_lo"], grid["y"], grid["z_hi"], grid["x"], lag_blocks)
     vmem = pl.BlockSpec(memory_space=pltpu.VMEM)
     dma = pltpu.SemaphoreType.DMA
-    return pl.pallas_call(
+    hbm = pl.BlockSpec(memory_space=pltpu.HBM)
+    landed = pl.pallas_call(
         functools.partial(kernel, dims, scale),
         out_shape=(
+            jax.ShapeDtypeStruct((n_ctx, ROWS, TOK), F32),
             jax.ShapeDtypeStruct((tokens, channels), F32),
-            jax.ShapeDtypeStruct((tokens, channels), F32),
-            jax.ShapeDtypeStruct((groups, lag_count // n_ctx), F32),
+            jax.ShapeDtypeStruct((n_ctx, 1, TOK), F32),
         ),
-        in_specs=[pl.BlockSpec(memory_space=pltpu.HBM)] * 6,
-        out_specs=(vmem,) * 3,
+        in_specs=[hbm] * 6,
+        out_specs=(hbm,) * 3,
         scratch_shapes=[
             pltpu.VMEM((tokens, channels), F32),
             pltpu.VMEM((tokens, channels), F32),
@@ -306,19 +316,18 @@
             pltpu.VMEM((min(8, groups), lag_count), F32),
             pltpu.VMEM((n_ctx, out_weight.shape[1], channels), BF16),
             pltpu.VMEM((n_ch, tokens, channels), BF16),
+            pltpu.VMEM((tokens, channels), F32),
             pltpu.VMEM((n_ctx, ROWS, TOK), F32),
             pltpu.VMEM((2, chips, ROWS, TOK), F32),
             pltpu.VMEM((n_ctx, ROWS, TOK), F32),
             pltpu.VMEM((2, chips + lag_blocks, ROWS, TOK), F32),
             pltpu.VMEM((2, chips, ROWS, TOK), F32),
-            pltpu.VMEM((n_ctx, ROWS, TOK), F32),
             pltpu.VMEM((BLOCK, wide), BF16),
             pltpu.VMEM((BLOCK, wide), BF16),
             pltpu.VMEM((BLOCK, chips * ROWS), BF16),
             pltpu.VMEM((BLOCK, chips * ROWS), BF16),
             pltpu.VMEM((BLOCK, wide), F32),
             pltpu.VMEM((segments, 1, TOK), F32),
-            pltpu.VMEM((n_ctx, 1, TOK), F32),
             pltpu.VMEM((tokens, channels), F32),
             dma,
             dma((n_ctx,)),
@@ -334,6 +343,17 @@
             collective_id=0, has_side_effects=True, vmem_limit_bytes=66_000_000
         ),
     )(cotangent, out_weight.T, gate_value, conv_output, conv_input, filters)
+    return pl.pallas_call(
+        finish,
+        out_shape=(
+            jax.ShapeDtypeStruct((tokens, channels), F32),
+            jax.ShapeDtypeStruct((tokens, channels), F32),
+            jax.ShapeDtypeStruct((groups, lag_count // n_ctx), F32),
+        ),
+        in_specs=[vmem] * 3,
+        out_specs=(vmem,) * 3,
+        compiler_params=pltpu.CompilerParams(vmem_limit_bytes=66_000_000),
+    )(*landed)
 
 
 def solution(mesh, grid=GRID):

time: 71.4 us -> 69.5 us (0.973)
  local copies, waits for them, and re-layouts: 3.04 us -> 0 us
  Pallas kernels: 67.5 us -> 68.7 us
    unnamed x7 -> x0, local copies, waits for them, and re-layouts: 3.04 us -> none
    pallas_call x0 -> x1, Pallas kernels: none -> 1.91 us  [shards(): pl.pallas_call(finish, out_shape=(jax.ShapeDtypeStruct((tokens, channels)...]
    pallas_call x1, Pallas kernels: 67.5 us -> 66.8 us  [shards(): pl.pallas_call(functools.partial(kernel, dims, scale), out_shape=(jax.Sha...]
where the time goes in v4:
time: 69.5 us; the launch traced here: 69.3 us
  Pallas kernels  68.7 us (99%)
    pallas_call x1, Pallas kernels, shards(): pl.pallas_call(functools.partial(kernel, dims, scale), out_shape=(jax.Sha...  66.8 us
    pallas_call x1, Pallas kernels, shards(): pl.pallas_call(finish, out_shape=(jax.ShapeDtypeStruct((tokens, channels)...  1.91 us

profile of v4, /device:TPU:1, one launch (start us, length us, event | category | flops | bytes accessed | tf_op | source)
XLA Modules:
  0.0 69.3 jit_solution(4563027284186091380)
XLA Ops:
  0.6 66.8 %shard_map.85 = (f32[64,8,128]{2,1,0:T(8,128)}, f32[128,512]{1,0:T(8,128)}, f32[64,1,128]{2,1,0:T(1,128)}) custom-call(bf16[128,512]{1,0:T(8,128)(2,1)} %cot_hbm.1, bf16[64,512]{1,0:T(8,128)(2,1)} %bitcast.1, f32[128,512]{1,0:T(8,128)} %gate_hbm.1, f32[128,512]{1,0:T(8,128)} %cout_hbm.1, f32[128,512]{1,0:T(8,128)} %cin_hbm.1, f32[32,2048]{1,0:T(8,128)} %filt_hbm.1), custom_call_target="tpu_custom_call" | custom-call | tf_op jit(solution)/shard_map/pallas_call | solution.py:303
  67.4 1.9 %shard_map.86 = (f32[128,512]{1,0:T(8,128)}, f32[128,512]{1,0:T(8,128)}, f32[32,32]{1,0:T(8,128)}) custom-call(f32[64,8,128]{2,1,0:T(8,128)} %get-tuple-element.6.rt, f32[128,512]{1,0:T(8,128)} %get-tuple-element.7.gg_in, f32[64,1,128]{2,1,0:T(1,128)} %get-tuple-element.8.fgr), custom_call_target="tpu_custom_call" | custom-call | tf_op jit(solution)/shard_map/pallas_call | solution.py:346

commit v5 on v4

--- a/solution.py
+++ b/solution.py
@@ -36,10 +36,11 @@
     cot_hbm, w_hbm, gate_hbm, cout_hbm, cin_hbm, filt_hbm,
     rt, gg_hbm, fgr,
     gate_ref, cout_ref, cin_ref, filt_ref, wfull, cotfull, gg_ref, xt, xb, st, sb, outt, tap_hi, tap_lo, xr_hi, xr_lo, corr, fgs, grad,
-    w_send, w_recv, c_send, c_recv, x_sem, s_sem, o_sem, f_sem, in_sem,
+    w_send, w_recv, b_send, b_recv, c_send, c_recv, x_sem, s_sem, o_sem, f_sem, in_sem,
 ):
     zl_n, y_n, zh_n, x_n, lag_blocks = dims
     chips = zl_n * y_n
+    depth = w_hbm.shape[0]
     n_ctx = 2 * chips
     me = lax.axis_index("ctx")
     core = lax.rem(me, 2)
@@ -78,7 +79,8 @@
     z_of = [lax.rem(zl + k, zl_n) for k in range(zl_n)]
     y_of = [lax.rem(y + k, y_n) for k in range(y_n)]
     up, down = (ctx_of(zl, y_of[k % y_n], core) for k in (1, y_n - 1))
-    rings = [sibling] + ([up, down] if y_n > 2 else [up] * (y_n > 1)) + [ctx_of(z, y, core) for z in z_of[1:]]
+    y_far = sorted(range(1, y_n), key=lambda k: -min(k, y_n - k))
+    rings = [sibling] + [ctx_of(zl, y_of[k], core) for k in y_far] + [ctx_of(z, y, core) for z in z_of[1:]]
     for near in rings:
         pl.semaphore_signal(barrier, inc=1, device_id={"ctx": near}, device_id_type=MESH)
     for near in x_far:
@@ -93,7 +95,7 @@
         for n, (src, dst) in enumerate(
             (
                 (cin_hbm, cin_ref),
-                (w_hbm, wfull.at[me]),
+                (w_hbm, wfull.at[zl, y, core]),
                 (cot_hbm, cotfull.at[mej]),
                 (filt_hbm.at[pl.ds(lax.div(group, some) * some, some)], filt_ref),
                 (gate_hbm, gate_ref),
@@ -106,12 +108,15 @@
     sb[:, chips:] = jnp.zeros((2, lag_blocks, ROWS, TOK), F32)
     loads[1].wait()
     loads[2].wait()
-    depth = w_hbm.shape[0]
 
     pl.semaphore_wait(barrier, len(rings) + len(x_far) + (zh_n - 1))
 
-    def w_copy(piece, target):
-        return remote(wfull.at[piece], wfull.at[piece], w_send, w_recv.at[piece], ctx=target)
+    main = pl.ds(0, depth - depth // 8)
+    rest = pl.ds(depth - depth // 8, depth // 8)
+
+    def w_copy(z_, y_, c_, target):
+        piece = wfull.at[z_, y_, c_, main]
+        return remote(piece, piece, w_send, w_recv.at[z_, y_, c_], ctx=target)
 
     def goes_up(distance, k):
         return distance < half or (distance == half and k < zl_n // 2)
@@ -119,16 +124,27 @@
     def goes_down(distance, k):
         return distance < half or (distance == half and k >= zl_n // 2)
 
-    def w_relay(piece, distance, k, to_up, to_down):
+    def w_relay(z_, y_, distance, k, to_up, to_down):
         if to_up and goes_up(distance, k):
-            w_copy(piece, up).start()
+            w_copy(z_, y_, core, up).start()
         if to_down and goes_down(distance, k):
-            w_copy(piece, down).start()
-        w_copy(piece, sibling).start()
+            w_copy(z_, y_, core, down).start()
+        w_copy(z_, y_, core, sibling).start()
 
     for k in range(1, zl_n):
-        w_copy(me, ctx_of(z_of[k], y, core)).start()
-    w_relay(me, 1, 0, y_n > 1, y_n > 1)
+        w_copy(zl, y, core, ctx_of(z_of[k], y, core)).start()
+    w_relay(zl, y, 1, 0, y_n > 1, y_n > 1)
+
+    def rest_y(y_, target):
+        rows = wfull.at[zl, y_, core, rest]
+        return remote(rows, rows, b_send, b_recv.at[y_], ctx=target)
+
+    def rest_z(z_, c_, target):
+        rows = wfull.at[z_, :, c_, rest]
+        return remote(rows, rows, b_send, b_recv.at[y_n + 2 * z_ + c_], ctx=target)
+
+    for k in y_far:
+        rest_y(y, ctx_of(zl, y_of[k], core)).start()
 
     def c_copy(piece, xx):
         return remote(cotfull.at[piece], cotfull.at[piece], c_send, c_recv.at[piece], ch=zh * x_n + xx)
@@ -141,19 +157,16 @@
     c_spread(mej)
 
     def from_z(k):
-        piece = ctx_of(z_of[k], y, core)
-        w_copy(piece, sibling).wait_recv()
-        w_relay(piece, 1, k, y_n > 1, y_n > 1)
+        w_copy(z_of[k], y, core, sibling).wait_recv()
+        w_relay(z_of[k], y, 1, k, y_n > 1, y_n > 1)
 
     def from_y(s, k):
         if goes_up(s, k):
-            piece = ctx_of(z_of[k], y_of[y_n - s], core)
-            w_copy(piece, sibling).wait_recv()
-            w_relay(piece, s + 1, k, True, False)
+            w_copy(z_of[k], y_of[y_n - s], core, sibling).wait_recv()
+            w_relay(z_of[k], y_of[y_n - s], s + 1, k, True, False)
         if goes_down(s, k):
-            piece = ctx_of(z_of[k], y_of[s], core)
-            w_copy(piece, sibling).wait_recv()
-            w_relay(piece, s + 1, k, False, True)
+            w_copy(z_of[k], y_of[s], core, sibling).wait_recv()
+            w_relay(z_of[k], y_of[s], s + 1, k, False, True)
 
     if half:
         from_y(1, 0)
@@ -174,9 +187,18 @@
             from_y(s + 1, 0)
         for k in range(1, zl_n):
             from_y(s, k)
+        if s == 1:
+            for k in y_far:
+                rest_y(y_of[k], sibling).wait_recv()
+            for z_ in z_of[1:]:
+                rest_z(zl, core, ctx_of(z_, y, core)).start()
+            rest_z(zl, core, sibling).start()
         if zh_n > 1 and s == 1:
             c_copy(across, x).wait_recv()
             c_spread(across)
+    for z_ in z_of[1:]:
+        rest_z(z_, core, sibling).wait_recv()
+        rest_z(z_, core, sibling).start()
     for piece in range(zh_n * x_n):
         first = lax.rem(mej + piece, zh_n * x_n)
         if piece and zh_n > 1:
@@ -186,15 +208,17 @@
         elif piece:
             c_copy(first, x).wait_recv()
 
-    def from_sibling(q, carry):
-        w_copy(2 * q + 1 - core, sibling).wait_recv()
-        return carry
-
-    lax.fori_loop(0, chips, from_sibling, 0)
+    for z_ in range(zl_n):
+        rest_z(z_, 1 - core, sibling).wait_recv()
+        for y_ in range(y_n):
+            w_copy(z_, y_, 1 - core, sibling).wait_recv()
 
     per = n_ctx // (zh_n * x_n)
     for j in range(zh_n * x_n):
-        term = mm(cotfull[j], wfull[pl.ds(j * per, per)].reshape(per * depth, wfull.shape[2]), NN)
+        z_, y_ = divmod(j * per // 2, y_n)
+        whole = per // 2 % y_n == 0
+        rows = wfull[z_ : z_ + per // 2 // y_n] if whole else wfull[z_, y_ : y_ + per // 2]
+        term = mm(cotfull[j], rows.reshape(per * depth, wfull.shape[4]), NN)
         if j == 0:
             grad[...] = term
         else:
@@ -267,7 +291,14 @@
     pltpu.make_async_copy(rt, rt, o_sem.at[1]).wait()
     pltpu.make_async_copy(fgr, fgr, f_sem.at[1]).wait()
 
-    pltpu.make_async_copy(wfull.at[pl.ds(0, n_ctx - 1)], wfull.at[pl.ds(0, n_ctx - 1)], w_send).wait()
+    left = [(w_send, wfull.at[0, 0, 0, main])]
+    if y_n > 1:
+        left += [(w_send, wfull.at[0, pl.ds(0, y_n - 1), :, main]), (b_send, wfull.at[0, pl.ds(0, y_n - 1), 0, rest])]
+    if zl_n > 1:
+        left += [(w_send, wfull.at[pl.ds(0, zl_n - 1), :, :, main]), (b_send, wfull.at[pl.ds(0, zl_n - 1), :, 0, rest])]
+    left += [(b_send, wfull.at[:, :, 0, rest])]
+    for sem, part in left:
+        pltpu.make_async_copy(part, part, sem).wait()
     if zh_n * x_n > 1:
         sent = cotfull.at[pl.ds(0, zh_n * x_n - 1)]
         pltpu.make_async_copy(sent, sent, c_send).wait()
@@ -314,7 +345,7 @@
             pltpu.VMEM((tokens, channels), F32),
             pltpu.VMEM((tokens, channels), F32),
             pltpu.VMEM((min(8, groups), lag_count), F32),
-            pltpu.VMEM((n_ctx, out_weight.shape[1], channels), BF16),
+            pltpu.VMEM((grid["z_lo"], grid["y"], 2, out_weight.shape[1], channels), BF16),
             pltpu.VMEM((n_ch, tokens, channels), BF16),
             pltpu.VMEM((tokens, channels), F32),
             pltpu.VMEM((n_ctx, ROWS, TOK), F32),
@@ -330,7 +361,9 @@
             pltpu.VMEM((segments, 1, TOK), F32),
             pltpu.VMEM((tokens, channels), F32),
             dma,
-            dma((n_ctx,)),
+            dma((grid["z_lo"], grid["y"], 2)),
+            dma,
+            dma((grid["y"] + 2 * grid["z_lo"],)),
             dma,
             dma((n_ch,)),
             dma((2,)),

time: 69.5 us -> 67.7 us (0.974)
  Pallas kernels: 68.7 us -> 66.9 us
    pallas_call x1, Pallas kernels: 66.8 us -> 64.9 us  [shards(): pl.pallas_call(functools.partial(kernel, dims, scale), out_shape=(jax.Sha...]
where the time goes in v5:
time: 67.7 us; the launch traced here: 67.5 us
  Pallas kernels  66.9 us (99%)
    pallas_call x1, Pallas kernels, shards(): pl.pallas_call(functools.partial(kernel, dims, scale), out_shape=(jax.Sha...  64.9 us
    pallas_call x1, Pallas kernels, shards(): pl.pallas_call(finish, out_shape=(jax.ShapeDtypeStruct((tokens, channels)...  1.91 us

profile of v5, /device:TPU:1, one launch (start us, length us, event | category | flops | bytes accessed | tf_op | source)
XLA Modules:
  0.0 67.5 jit_solution(5840391286507780296)
XLA Ops:
  0.6 64.9 %shard_map.85 = (f32[64,8,128]{2,1,0:T(8,128)}, f32[128,512]{1,0:T(8,128)}, f32[64,1,128]{2,1,0:T(1,128)}) custom-call(bf16[128,512]{1,0:T(8,128)(2,1)} %cot_hbm.1, bf16[64,512]{1,0:T(8,128)(2,1)} %bitcast.1, f32[128,512]{1,0:T(8,128)} %gate_hbm.1, f32[128,512]{1,0:T(8,128)} %cout_hbm.1, f32[128,512]{1,0:T(8,128)} %cin_hbm.1, f32[32,2048]{1,0:T(8,128)} %filt_hbm.1), custom_call_target="tpu_custom_call" | custom-call | tf_op jit(solution)/shard_map/pallas_call | solution.py:334
  65.6 1.9 %shard_map.86 = (f32[128,512]{1,0:T(8,128)}, f32[128,512]{1,0:T(8,128)}, f32[32,32]{1,0:T(8,128)}) custom-call(f32[64,8,128]{2,1,0:T(8,128)} %get-tuple-element.6.rt, f32[128,512]{1,0:T(8,128)} %get-tuple-element.7.gg_in, f32[64,1,128]{2,1,0:T(1,128)} %get-tuple-element.8.fgr), custom_call_target="tpu_custom_call" | custom-call | tf_op jit(solution)/shard_map/pallas_call | solution.py:379

commit v6 on v5

--- a/solution.py
+++ b/solution.py
@@ -35,7 +35,7 @@
     dims, scale,
     cot_hbm, w_hbm, gate_hbm, cout_hbm, cin_hbm, filt_hbm,
     rt, gg_hbm, fgr,
-    gate_ref, cout_ref, cin_ref, filt_ref, wfull, cotfull, gg_ref, xt, xb, st, sb, outt, tap_hi, tap_lo, xr_hi, xr_lo, corr, fgs, grad,
+    gate_ref, cout_ref, cin_ref, filt_ref, wfull, cotfull, gg_ref, xt, xb, st, sb, outt, tap_hi, tap_lo, xr_hi, xr_lo, corr, s_hi, s_lo, fgs, grad,
     w_send, w_recv, b_send, b_recv, c_send, c_recv, x_sem, s_sem, o_sem, f_sem, in_sem,
 ):
     zl_n, y_n, zh_n, x_n, lag_blocks = dims
@@ -105,6 +105,7 @@
     ]
     for load in loads:
         load.start()
+    wide = tap_hi.shape[1]
     sb[:, chips:] = jnp.zeros((2, lag_blocks, ROWS, TOK), F32)
     loads[1].wait()
     loads[2].wait()
@@ -174,14 +175,6 @@
         from_z(k)
     if zh_n > 1:
         remote(cotfull.at[mej], cotfull.at[mej], c_send, c_recv.at[mej], ch=across).start()
-    loads[3].wait()
-    wide = tap_hi.shape[1]
-    row = jnp.pad(filt_ref[pl.ds(lax.rem(group, some), 1), :], ((0, 0), (0, wide - filt_ref.shape[1])))
-    taps = pltpu.roll(jnp.broadcast_to(row, (BLOCK, wide)), 0, 1, stride=1, stride_axis=0)
-    tap_hi[...], tap_lo[...] = split(taps)
-
-    loads[0].wait()
-    xt[...] = jnp.transpose(cin_ref[...]).reshape(n_ctx, ROWS, TOK)
     for s in range(1, half + 1):
         if s < half:
             from_y(s + 1, 0)
@@ -193,6 +186,15 @@
             for z_ in z_of[1:]:
                 rest_z(zl, core, ctx_of(z_, y, core)).start()
             rest_z(zl, core, sibling).start()
+        if s == min(2, half):
+            loads[3].wait()
+            wide = tap_hi.shape[1]
+            row = jnp.pad(filt_ref[pl.ds(lax.rem(group, some), 1), :], ((0, 0), (0, wide - filt_ref.shape[1])))
+            taps = pltpu.roll(jnp.broadcast_to(row, (BLOCK, wide)), 0, 1, stride=1, stride_axis=0)
+            tap_hi[...], tap_lo[...] = split(taps)
+
+            loads[0].wait()
+            xt[...] = jnp.transpose(cin_ref[...]).reshape(n_ctx, ROWS, TOK)
         if zh_n > 1 and s == 1:
             c_copy(across, x).wait_recv()
             c_spread(across)
@@ -252,7 +254,8 @@
     blocks = [slice(d * BLOCK, (d + 1) * BLOCK) for d in range(lag_blocks + 1)]
     total = jnp.zeros((chips * ROWS, BLOCK), F32)
     for d, cols in enumerate(blocks):
-        total = total + mm3(s_rows(d), (tap_hi[:, cols], tap_lo[:, cols]), NT)
+        s_hi[d], s_lo[d] = pair = s_rows(d)
+        total = total + mm3(pair, (tap_hi[:, cols], tap_lo[:, cols]), NT)
     for c in range(2):
         outt[c] = total[:, c * TOK : (c + 1) * TOK].reshape(chips, ROWS, TOK)
 
@@ -272,9 +275,10 @@
     xr_lo[...] = mm(turn, x_lo, NT).astype(BF16)
 
     for d, cols in enumerate(blocks):
-        corr[:, cols] = mm3((xr_hi[...], xr_lo[...]), s_rows(d), NN)
-
-    lined = pltpu.roll(corr[...], wide - (BLOCK - 1), 1, stride=1, stride_axis=0)
+        corr[:, cols] = mm3((xr_hi[...], xr_lo[...]), (s_hi[d], s_lo[d]), NN)
+
+    folded = corr[TOK:, : wide - TOK] + corr[:TOK, TOK:]
+    lined = pltpu.roll(folded, wide - TOK - (TOK - 1), 1, stride=1, stride_axis=0)
     lags = jnp.sum(lined, axis=0, keepdims=True) * scale
     for s in range(fgs.shape[0]):
         fgs[s] = lags[:, s * TOK : (s + 1) * TOK]
@@ -358,6 +362,8 @@
             pltpu.VMEM((BLOCK, chips * ROWS), BF16),
             pltpu.VMEM((BLOCK, chips * ROWS), BF16),
             pltpu.VMEM((BLOCK, wide), F32),
+            pltpu.VMEM((lag_blocks + 1, chips * ROWS, BLOCK), BF16),
+            pltpu.VMEM((lag_blocks + 1, chips * ROWS, BLOCK), BF16),
             pltpu.VMEM((segments, 1, TOK), F32),
             pltpu.VMEM((tokens, channels), F32),
             dma,

time: 67.7 us -> 67.7 us (level)
  no operation moved by 1% of the time
where the time goes in v6:
time: 67.7 us; the launch traced here: 67.5 us
  Pallas kernels  66.9 us (99%)
    pallas_call x1, Pallas kernels, shards(): pl.pallas_call(functools.partial(kernel, dims, scale), out_shape=(jax.Sha...  64.9 us
    pallas_call x1, Pallas kernels, shards(): pl.pallas_call(finish, out_shape=(jax.ShapeDtypeStruct((tokens, channels)...  1.91 us

profile of v6, /device:TPU:1, one launch (start us, length us, event | category | flops | bytes accessed | tf_op | source)
XLA Modules:
  0.0 67.5 jit_solution(1313466623998558698)
XLA Ops:
  0.6 64.9 %shard_map.85 = (f32[64,8,128]{2,1,0:T(8,128)}, f32[128,512]{1,0:T(8,128)}, f32[64,1,128]{2,1,0:T(1,128)}) custom-call(bf16[128,512]{1,0:T(8,128)(2,1)} %cot_hbm.1, bf16[64,512]{1,0:T(8,128)(2,1)} %bitcast.1, f32[128,512]{1,0:T(8,128)} %gate_hbm.1, f32[128,512]{1,0:T(8,128)} %cout_hbm.1, f32[128,512]{1,0:T(8,128)} %cin_hbm.1, f32[32,2048]{1,0:T(8,128)} %filt_hbm.1), custom_call_target="tpu_custom_call" | custom-call | tf_op jit(solution)/shard_map/pallas_call | solution.py:338
  65.6 1.9 %shard_map.86 = (f32[128,512]{1,0:T(8,128)}, f32[128,512]{1,0:T(8,128)}, f32[32,32]{1,0:T(8,128)}) custom-call(f32[64,8,128]{2,1,0:T(8,128)} %get-tuple-element.6.rt, f32[128,512]{1,0:T(8,128)} %get-tuple-element.7.gg_in, f32[64,1,128]{2,1,0:T(1,128)} %get-tuple-element.8.fgr), custom_call_target="tpu_custom_call" | custom-call | tf_op jit(solution)/shard_map/pallas_call | solution.py:385
